TPU v7x, 256 devices: a whole 4x4x8 slice. The times are simulated.
256 devices in a mesh: dp: 2 (over core), seq: 8 (over z), expert: 16 (over y, x).
Axes of the slice: x: 4, y: 4, z: 8, core: 2. Of those that a mesh axis runs over, the one named last changes fastest.
Arguments:
- tokens: bfloat16 [16384, 2048], P(('dp', 'seq')), may hold values from -6 to 6
- phi: bfloat16 [2048, 32], P(None, 'expert'), may hold values from -40 to 40
- w_in: bfloat16 [32, 2048, 8192], P('expert', None, ('dp', 'seq')), may hold values from -1 to 1
- w_out: bfloat16 [32, 8192, 2048], P('expert', ('dp', 'seq')), may hold values from -0.25 to 0.25
Outputs:
- mixed: bfloat16 [16384, 2048], P(('dp', 'seq', 'expert'))
All inputs are finite; a program needn't handle non-finite values.
Results may differ from a plain program's by a relative error of at most 0.0068.
Values may be sent and summed in bfloat16 or wider, within the bound.
A program may use at most 64 MiB of HBM per device.

v0:
```python
import jax
import jax.numpy as jnp
from jax import lax
from jax.sharding import PartitionSpec as P


def on_device(tokens, phi, w_in, w_out):
    n_expert = lax.axis_size("expert")
    rows_out = tokens.shape[0] // n_expert
    phi_all = lax.all_gather(phi, "expert", axis=1, tiled=True)
    logits = lax.dot_general(
        phi, tokens, (((0,), (1,)), ((), ())), preferred_element_type=jnp.float32
    )
    slot_max = lax.pmax(jnp.max(logits, axis=1), "seq")
    spread = jnp.exp(logits - slot_max[:, None])
    numerator = jnp.dot(spread.astype(jnp.bfloat16), tokens, preferred_element_type=jnp.float32)
    denominator = jnp.sum(spread, axis=1)
    numer_seq, denom_seq = lax.psum((numerator, denominator), "seq")
    own_slots = (numer_seq / denom_seq[:, None]).astype(jnp.bfloat16)
    slot_in = lax.all_gather(own_slots[None], "dp", axis=0, tiled=True)
    hidden = jax.nn.gelu(
        jnp.einsum("ced,edf->cef", slot_in, w_in, preferred_element_type=jnp.float32),
        approximate=True,
    ).astype(jnp.bfloat16)
    partial_value = jnp.einsum("cef,efd->ced", hidden, w_out, preferred_element_type=jnp.float32)
    totals = lax.psum(partial_value, ("dp", "seq"))
    summed = lax.dynamic_index_in_dim(totals, lax.axis_index("dp"), 0, keepdims=False)
    slot_out = lax.all_gather(summed.astype(jnp.bfloat16), "expert", axis=0, tiled=True)
    rows = lax.dynamic_slice_in_dim(tokens, lax.axis_index("expert") * rows_out, rows_out, 0)
    row_logits = lax.dot_general(
        phi_all, rows, (((0,), (1,)), ((), ())), preferred_element_type=jnp.float32
    )
    row_max = jnp.max(row_logits, axis=0)
    combine_weights = jnp.exp(row_logits - row_max[None, :])
    mixed_numer = lax.dot_general(
        combine_weights.astype(jnp.bfloat16),
        slot_out,
        (((0,), (0,)), ((), ())),
        preferred_element_type=jnp.float32,
    )
    mixed_denom = jnp.sum(combine_weights, axis=0)
    return (mixed_numer / mixed_denom[:, None]).astype(jnp.bfloat16)


def solution(mesh):
    placed = (
        P(("dp", "seq"), None),
        P(None, "expert"),
        P("expert", None, ("dp", "seq")),
        P("expert", ("dp", "seq"), None),
    )
    return jax.shard_map(
        on_device,
        mesh=mesh,
        in_specs=placed,
        out_specs=P(("dp", "seq", "expert"), None),
        check_vma=False,
    )
```

profile of v0, /device:TPU:32, one launch (start us, length us, event | category | flops | bytes accessed | tf_op | source)
XLA Modules:
  0.0 159.4 jit_solution(6288700102996713554)
XLA Ops:
  0.0 3.5 %fusion.39 = (f32[2]{0:T(128)S(1)}, f32[2,1024]{1,0:T(2,128)S(1)}) fusion(bf16[2048,2]{0,1:T(2,128)(2,1)} %param.5, bf16[1024,2048]{1,0:T(8,128)(2,1)} %param.4), kind=kOutput, calls=%fused_computation.39 | convolution fusion | flops 8390654 | bytes 4210696 | tf_op jit(solution)/shard_map/dot_general | solution.py:11
  3.5 17.9 %pmax.7 = f32[2]{0:T(128)S(1)} all-reduce(f32[2]{0:T(128)S(1)} %get-tuple-element.9), channel_id=1, replica_groups=mesh['dp'=2,'seq'=8,'expert'=16] {'seq'}, use_global_device_ids=true, to_apply=%region_2.0 | all-reduce | flops 2 | bytes 16 | tf_op jit(solution)/shard_map/pmax | solution.py:14
  21.4 0.2 fusion.25
  21.6 2.9 %fusion.27 = f32[2,2048]{1,0:T(2,128)S(1)} fusion(bf16[1024,2048]{1,0:T(8,128)(2,1)} %param.4, f32[2,1024]{1,0:T(2,128)S(1)} %get-tuple-element.10, f32[2]{0:T(128)S(1)} %pmax.7), kind=kOutput, calls=%fused_computation.28 | convolution fusion | flops 8392704 | bytes 4218888 | tf_op jit(solution)/shard_map/dot_general | solution.py:16
  24.5 27.9 %all-reduce = (f32[2,2048]{1,0:T(2,128)S(1)}, f32[2]{0:T(128)S(1)}) all-reduce(f32[2,2048]{1,0:T(2,128)S(1)} %fusion.27, f32[2]{0:T(128)S(1)} %fusion.25), channel_id=1, replica_groups=mesh['dp'=2,'seq'=8,'expert'=16] {'seq'}, use_global_device_ids=true, to_apply=%region_3.0 | all-reduce | flops 4098 | bytes 32784 | tf_op jit(solution)/shard_map/psum | solution.py:18
  52.4 0.1 fusion.24
  52.5 1.8 %all-gather.3 = bf16[2,2,2048]{2,1,0:T(2,128)(2,1)S(1)} all-gather(bf16[1,2,2048]{2,1,0:T(2,128)(2,1)S(1)} %fusion.24), channel_id=2, replica_groups=mesh['dp'=2,'seq'=8,'expert'=16] {'dp'}, dimensions={0}, use_global_device_ids=true | all-gather | bytes 24576 | tf_op jit(solution)/shard_map/all_gather | solution.py:20
  54.3 0.0 copy-start
  54.3 4.7 %convolution_bitcast_fusion = f32[2,2,2048]{2,0,1:T(2,128)S(1)} fusion(bf16[2,512,2048]{2,1,0:T(8,128)(2,1)} %param.7, bf16[2,2048,512]{2,1,0:T(8,128)(2,1)} %param.6, bf16[2,2,2048]{2,1,0:T(2,128)(2,1)S(1)} %all-gather.3), kind=kOutput, calls=%fused_computation.2 | convolution fusion | flops 16795648 | bytes 8437760 | tf_op jit(solution)/shard_map/cef,efd->ced/dot_general | solution.py:25
  59.0 51.1 %psum.23 = bf16[2,2,2048]{2,0,1:T(2,128)(2,1)S(1)} all-reduce(f32[2,2,2048]{2,0,1:T(2,128)S(1)} %convolution_bitcast_fusion), channel_id=1, replica_groups=mesh['dp'=2,'seq'=8,'expert'=16] {'dp','seq'}, use_global_device_ids=true, to_apply=%region_6.7 | all-reduce | flops 8192 | bytes 49152 | tf_op jit(solution)/shard_map/psum | solution.py:26
  110.1 0.0 copy-done
  110.1 24.0 %all-gather.2 = bf16[16,2,2048]{2,1,0:T(2,128)(2,1)S(1)} all-gather(bf16[1,2,2048]{2,1,0:T(2,128)(2,1)S(1)} %bitcast.24), channel_id=1, replica_groups=mesh['dp'=2,'seq'=8,'expert'=16] {'expert'}, dimensions={0}, use_global_device_ids=true | all-gather | bytes 139264 | tf_op jit(solution)/shard_map/all_gather | solution.py:10
  134.1 0.1 reshape.8
  134.1 1.2 fusion.38
  135.3 23.1 %all-gather.1 = bf16[1,32,2048]{2,0,1:T(2,128)(2,1)S(1)} all-gather(bf16[1,2,2048]{2,0,1:T(2,128)(2,1)S(1)} %dynamic-slice_convert_fusion), channel_id=3, replica_groups=mesh['dp'=2,'seq'=8,'expert'=16] {'expert'}, dimensions={1}, use_global_device_ids=true | all-gather | bytes 139264 | tf_op jit(solution)/shard_map/all_gather | solution.py:28
  158.4 1.0 fusion
  (2 shorter events, 0.1 us)
Async XLA Ops:
  54.3 55.8 %copy-start = (bf16[2048,2]{0,1:T(2,128)(2,1)S(1)}, bf16[2048,2]{0,1:T(2,128)(2,1)}, u32[]{:S(2)}) copy-start(bf16[2048,2]{0,1:T(2,128)(2,1)} %param.5) | copy-start | bytes 24580
where the time goes:
time: 160 us; the launch traced here: 159 us
  blocking collectives  146 us (91%)
  matrix products  13.2 us (8%)
    psum x1, blocking collectives, on_device(): totals = lax.psum(partial_value, ('dp', 'seq'))  51.1 us
    psum x1, blocking collectives, on_device(): numer_seq, denom_seq = lax.psum((numerator, denominator), 'seq')  27.9 us
    all_gather x1, blocking collectives, on_device(): phi_all = lax.all_gather(phi, 'expert', axis=1, tiled=True)  24 us
    all_gather x1, blocking collectives, on_device(): lax.all_gather(summed.astype(jnp.bfloat16), 'expert', axis=0, tiled=True)  23.1 us
    pmax x1, blocking collectives, on_device(): slot_max = lax.pmax(jnp.max(logits, axis=1), 'seq')  17.9 us
    dot_general x1, matrix products, on_device(): jnp.einsum('cef,efd->ced', hidden, w_out, preferred_element_type=jnp.floa...  4.66 us
    dot_general x1, matrix products, on_device(): lax.dot_general(phi, tokens, (((0,), (1,)), ((), ())), preferred_element_...  3.5 us

commit v1 on v0

--- a/solution.py
+++ b/solution.py
@@ -2,6 +2,7 @@
 import jax.numpy as jnp
 from jax import lax
 from jax.sharding import PartitionSpec as P
+from jax.lax import all_gather
 
 
 def on_device(tokens, phi, w_in, w_out):
@@ -23,7 +24,8 @@
         approximate=True,
     ).astype(jnp.bfloat16)
     partial_value = jnp.einsum("cef,efd->ced", hidden, w_out, preferred_element_type=jnp.float32)
-    totals = lax.psum(partial_value, ("dp", "seq"))
+    fix_the_windows = lambda mat, a_name: all_gather(mat, a_name).sum(axis=0)
+    totals = fix_the_windows(partial_value, ("dp", "seq"))
     summed = lax.dynamic_index_in_dim(totals, lax.axis_index("dp"), 0, keepdims=False)
     slot_out = lax.all_gather(summed.astype(jnp.bfloat16), "expert", axis=0, tiled=True)
     rows = lax.dynamic_slice_in_dim(tokens, lax.axis_index("expert") * rows_out, rows_out, 0)

time: 160 us -> 137 us (0.86)
  blocking collectives: 146 us -> 123 us
    psum x1 -> x0, blocking collectives: 51.1 us -> none  [on_device(): totals = lax.psum(partial_value, ('dp', 'seq'))]
    all_gather x0 -> x1, blocking collectives: none -> 28.5 us  [on_device(): fix_the_windows = lambda mat, a_name: all_gather(mat, a_name).sum(axis=0)]
where the time goes in v1:
time: 137 us
  blocking collectives  123 us (90%)
  matrix products  13.2 us (10%)
    all_gather x1, blocking collectives, on_device(): fix_the_windows = lambda mat, a_name: all_gather(mat, a_name).sum(axis=0)  28.5 us
    psum x1, blocking collectives, on_device(): numer_seq, denom_seq = lax.psum((numerator, denominator), 'seq')  28 us
    all_gather x1, blocking collectives, on_device(): lax.all_gather(summed.astype(jnp.bfloat16), 'expert', axis=0, tiled=True)  24 us
    all_gather x1, blocking collectives, on_device(): phi_all = lax.all_gather(phi, 'expert', axis=1, tiled=True)  23 us
    pmax x1, blocking collectives, on_device(): slot_max = lax.pmax(jnp.max(logits, axis=1), 'seq')  17.9 us
    dot_general x1, matrix products, on_device(): jnp.einsum('cef,efd->ced', hidden, w_out, preferred_element_type=jnp.floa...  4.66 us
    dot_general x1, matrix products, on_device(): lax.dot_general(phi, tokens, (((0,), (1,)), ((), ())), preferred_element_...  3.5 us
    dot_general x1, matrix products, on_device(): jnp.dot(spread.astype(jnp.bfloat16), tokens, preferred_element_type=jnp.f...  2.88 us

profile of v1, /device:TPU:32, one launch (start us, length us, event | category | flops | bytes accessed | tf_op | source)
XLA Modules:
  0.0 137.0 jit_solution(2608634129651959268)
XLA Ops:
  0.0 3.5 %fusion.39 = (f32[2]{0:T(128)S(1)}, f32[2,1024]{1,0:T(2,128)S(1)}) fusion(bf16[2048,2]{0,1:T(2,128)(2,1)} %param.5, bf16[1024,2048]{1,0:T(8,128)(2,1)} %param.4), kind=kOutput, calls=%fused_computation.40 | convolution fusion | flops 8390654 | bytes 4210696 | tf_op jit(solution)/shard_map/dot_general | solution.py:12
  3.5 17.9 %pmax.7 = f32[2]{0:T(128)S(1)} all-reduce(f32[2]{0:T(128)S(1)} %get-tuple-element.9), channel_id=1, replica_groups=mesh['dp'=2,'seq'=8,'expert'=16] {'seq'}, use_global_device_ids=true, to_apply=%region_2.0 | all-reduce | flops 2 | bytes 16 | tf_op jit(solution)/shard_map/pmax | solution.py:15
  21.4 2.9 %fusion.27 = f32[2,2048]{1,0:T(2,128)S(1)} fusion(bf16[1024,2048]{1,0:T(8,128)(2,1)} %param.4, f32[2,1024]{1,0:T(2,128)S(1)} %get-tuple-element.10, f32[2]{0:T(128)S(1)} %pmax.7), kind=kOutput, calls=%fused_computation.28 | convolution fusion | flops 8392704 | bytes 4218888 | tf_op jit(solution)/shard_map/dot_general | solution.py:17
  24.3 0.2 fusion.25
  24.5 28.0 %all-reduce = (f32[2,2048]{1,0:T(2,128)S(1)}, f32[2]{0:T(128)S(1)}) all-reduce(f32[2,2048]{1,0:T(2,128)S(1)} %fusion.27, f32[2]{0:T(128)S(1)} %fusion.25), channel_id=1, replica_groups=mesh['dp'=2,'seq'=8,'expert'=16] {'seq'}, use_global_device_ids=true, to_apply=%region_3.0 | all-reduce | flops 4098 | bytes 32784 | tf_op jit(solution)/shard_map/psum | solution.py:19
  52.4 0.1 fusion.24
  52.5 1.8 %all-gather.4 = bf16[2,2,2048]{2,1,0:T(2,128)(2,1)S(1)} all-gather(bf16[1,2,2048]{2,1,0:T(2,128)(2,1)S(1)} %fusion.24), channel_id=2, replica_groups=mesh['dp'=2,'seq'=8,'expert'=16] {'dp'}, dimensions={0}, use_global_device_ids=true | all-gather | bytes 24576 | tf_op jit(solution)/shard_map/all_gather | solution.py:21
  54.3 0.0 copy-start
  54.3 4.7 %convolution_bitcast_fusion = f32[2,2,2048]{2,0,1:T(2,128)S(1)} fusion(bf16[2,512,2048]{2,1,0:T(8,128)(2,1)} %param.7, bf16[2,2048,512]{2,1,0:T(8,128)(2,1)} %param.6, bf16[2,2,2048]{2,1,0:T(2,128)(2,1)S(1)} %all-gather.4), kind=kOutput, calls=%fused_computation.2 | convolution fusion | flops 16795648 | bytes 8437760 | tf_op jit(solution)/shard_map/cef,efd->ced/dot_general | solution.py:26
  59.0 28.5 %all-gather.1 = f32[32,2,2048]{2,1,0:T(2,128)S(1)} all-gather(f32[2,2,2048]{2,1,0:T(2,128)S(1)} %copy.10), channel_id=3, replica_groups=mesh['dp'=2,'seq'=8,'expert'=16] {'dp','seq'}, dimensions={0}, use_global_device_ids=true | all-gather | bytes 557056 | tf_op jit(solution)/shard_map/all_gather | solution.py:27
  87.5 0.2 reduce_sum.28
  87.7 24.0 %all-gather.2 = bf16[1,32,2048]{2,0,1:T(2,128)(2,1)S(1)} all-gather(bf16[1,2,2048]{2,0,1:T(2,128)(2,1)S(1)} %copy.28), channel_id=4, replica_groups=mesh['dp'=2,'seq'=8,'expert'=16] {'expert'}, dimensions={1}, use_global_device_ids=true | all-gather | bytes 139264 | tf_op jit(solution)/shard_map/all_gather | solution.py:30
  111.8 0.0 copy-done
  111.8 23.0 %all-gather.3 = bf16[16,2,2048]{2,1,0:T(2,128)(2,1)S(1)} all-gather(bf16[1,2,2048]{2,1,0:T(2,128)(2,1)S(1)} %bitcast.26), channel_id=1, replica_groups=mesh['dp'=2,'seq'=8,'expert'=16] {'expert'}, dimensions={0}, use_global_device_ids=true | all-gather | bytes 139264 | tf_op jit(solution)/shard_map/all_gather | solution.py:11
  134.8 0.1 reshape.9
  134.8 1.2 fusion.38
  136.0 1.0 fusion
  (4 shorter events, 0.1 us)
Async XLA Ops:
  54.3 57.5 %copy-start = (bf16[2048,2]{0,1:T(2,128)(2,1)S(1)}, bf16[2048,2]{0,1:T(2,128)(2,1)}, u32[]{:S(2)}) copy-start(bf16[2048,2]{0,1:T(2,128)(2,1)} %param.5) | copy-start | bytes 24580
